TPU v7x, 32 devices: a whole 2x2x4 slice. The times are simulated.
32 devices in a mesh: rep: 8 (over z, x), exp: 4 (over y, core).
Axes of the slice: x: 2, y: 2, z: 4, core: 2. Of those that a mesh axis runs over, the one named last changes fastest.
Arguments:
- expert_ids: int32 [8, 512, 8], P('rep', 'exp'), may hold values from 0 to 15, as said below
- route_weights: bfloat16 [8, 512, 8], P('rep', 'exp'), may hold values from 0.049804688 to 0.59765625
- out_grad: bfloat16 [8, 512, 1024], P('rep', 'exp'), may hold values from -6 to 6
- saved_inputs: bfloat16 [8, 4, 32, 1024], P('rep', 'exp'), may hold values from -6 to 6
- gate_weight: bfloat16 [4, 1024, 384], P('exp', 'rep'), may hold values from -0.1875 to 0.1875
- up_weight: bfloat16 [4, 1024, 384], P('exp', 'rep'), may hold values from -0.1875 to 0.1875
- down_weight: bfloat16 [4, 1024, 384], P('exp', 'rep'), may hold values from -0.3125 to 0.3125
Outputs:
- input_grad: bfloat16 [8, 512, 1024], P('rep', 'exp')
- route_grad: bfloat16 [8, 512, 8], P('rep', 'exp')
- gate_grad: float32 [4, 1024, 384], P('exp', 'rep')
- up_grad: float32 [4, 1024, 384], P('exp', 'rep')
- down_grad: float32 [4, 1024, 384], P('exp', 'rep')
Inputs may be any that keep to these rules, and one draw needn't show every extreme that they name: `expert_ids`: each row names 8 different experts. Within each aligned block of 128 rows of one replica, an expert e with e % 4 == 0 is named at most 8 times; for every replica, some such expert is named exactly 8 times in each of its blocks.
All inputs are finite; a program needn't handle non-finite values.
Results may differ from a plain program's by a relative error of at most 0.014.
Values may be sent and summed in bfloat16 or wider, within the bound.
No kernel may reach another device: no remote copies, remote signals or barrier semaphores. Data moves between devices by JAX's collectives and lax.ppermute only.
A program may use at most 64 MiB of HBM per device.

v0:
```python
import jax
import jax.numpy as jnp
from jax import lax
from jax.sharding import PartitionSpec as P

TOPK = 8
EXP_DEV = 4


def slot_table(block_ids, slot_count, owners):
    flat_ids = block_ids.reshape(-1)
    chosen = flat_ids % EXP_DEV == 0
    owner_of = flat_ids // EXP_DEV
    capacity = slot_count // owners
    onehot = ((owner_of[:, None] == jnp.arange(owners)[None, :]) & chosen[:, None]).astype(
        jnp.int32
    )
    earlier = jnp.cumsum(onehot, axis=0) - onehot
    position = jnp.sum(earlier * onehot, axis=1)
    slot_of = jnp.where(chosen, owner_of * capacity + position, -1)
    return slot_of[None, :] == jnp.arange(slot_count)[:, None]


def first_contract(left, right):
    return lax.dot_general(
        left, right, (((0,), (0,)), ((), ())), preferred_element_type=jnp.float32
    )


def second_contract(left, right):
    return lax.dot_general(
        left, right, (((1,), (1,)), ((), ())), preferred_element_type=jnp.float32
    )


def body(expert_ids, route_weights, out_grad, saved_inputs, gate_weight, up_weight, down_weight):
    owners = lax.axis_size("exp")
    replicas = lax.axis_size("rep")
    tokens_here = out_grad.shape[1]
    features = out_grad.shape[2]
    hidden_width = gate_weight.shape[2]
    slot_count = saved_inputs.shape[2]
    capacity = slot_count // owners
    placed = slot_table(expert_ids[0], slot_count, owners)
    weights_flat = route_weights[0].reshape(-1)
    slot_scale = jnp.sum(
        jnp.where(placed, weights_flat[None, :], jnp.zeros((), weights_flat.dtype)), axis=1
    )
    token_hits = jnp.any(placed.reshape(slot_count, tokens_here, TOPK), axis=2)
    token_of = jnp.sum(jnp.where(token_hits, jnp.arange(tokens_here)[None, :], 0), axis=1)
    is_live = jnp.any(token_hits, axis=1)
    routed = jnp.where(is_live[:, None], out_grad[0][token_of], jnp.zeros((), jnp.bfloat16))
    arrived, arrived_scale = (
        lax.all_to_all(
            routed.reshape(owners, capacity, features),
            "exp",
            split_axis=0,
            concat_axis=0,
            tiled=True,
        ),
        lax.all_to_all(
            slot_scale.reshape(owners, capacity), "exp", split_axis=0, concat_axis=0, tiled=True
        ),
    )
    full_gate, full_up, full_down = (
        lax.all_gather(gate_weight[0], "rep", axis=0, tiled=True),
        lax.all_gather(up_weight[0], "rep", axis=0, tiled=True),
        lax.all_gather(down_weight[0], "rep", axis=0, tiled=True),
    )
    grad_rows = arrived.reshape(slot_count, features)
    scale_col = arrived_scale.reshape(slot_count, 1).astype(jnp.float32)
    inputs_here = saved_inputs[0, 0]
    pre_gate = jnp.dot(inputs_here, full_gate, preferred_element_type=jnp.float32)
    pre_up = jnp.dot(inputs_here, full_up, preferred_element_type=jnp.float32)
    sigmoid_gate = jax.nn.sigmoid(pre_gate)
    activated = pre_gate * sigmoid_gate
    hidden = (activated * pre_up).astype(jnp.bfloat16)
    raw_grad = jnp.dot(grad_rows, full_down, preferred_element_type=jnp.float32)
    slot_route = jnp.sum(hidden.astype(jnp.float32) * raw_grad, axis=1).astype(jnp.bfloat16)
    hidden_grad = scale_col * raw_grad
    scaled_rows = (scale_col * grad_rows.astype(jnp.float32)).astype(jnp.bfloat16)
    gate_delta = (
        hidden_grad * pre_up * sigmoid_gate * (1.0 + pre_gate * (1.0 - sigmoid_gate))
    ).astype(jnp.bfloat16)
    up_delta = (hidden_grad * activated).astype(jnp.bfloat16)
    back_rows = (
        second_contract(gate_delta, full_gate) + second_contract(up_delta, full_up)
    ).astype(jnp.bfloat16)
    returned, returned_route = (
        lax.all_to_all(
            back_rows.reshape(owners, capacity, features),
            "exp",
            split_axis=0,
            concat_axis=0,
            tiled=True,
        ),
        lax.all_to_all(
            slot_route.reshape(owners, capacity), "exp", split_axis=0, concat_axis=0, tiled=True
        ),
    )
    returned_flat = returned.reshape(slot_count, features)
    route_flat = returned_route.reshape(slot_count)
    combined = jax.ops.segment_sum(
        jnp.where(is_live[:, None], returned_flat.astype(jnp.float32), 0.0),
        token_of,
        num_segments=tokens_here,
    )
    input_grad = combined.astype(jnp.bfloat16)[None]
    route_grad = jnp.sum(
        jnp.where(placed, route_flat[:, None], jnp.zeros((), jnp.bfloat16)), axis=0
    )
    route_grad = route_grad.reshape(1, tokens_here, TOPK)
    joined_share = lax.psum_scatter(
        jnp.concatenate(
            [
                jnp.concatenate(
                    [
                        first_contract(inputs_here, gate_delta),
                        first_contract(inputs_here, up_delta),
                    ],
                    axis=1,
                ),
                first_contract(scaled_rows, hidden),
            ],
            axis=1,
        ),
        "rep",
        scatter_dimension=0,
        tiled=True,
    )
    gate_share = joined_share[:, :hidden_width]
    up_share = joined_share[:, hidden_width : 2 * hidden_width]
    down_share = joined_share[:, 2 * hidden_width :]
    gate_grad = (gate_share / replicas)[None]
    up_grad = (up_share / replicas)[None]
    down_grad = (down_share / replicas)[None]
    return (input_grad, route_grad, gate_grad, up_grad, down_grad)


def solution(mesh):
    in_specs = (
        P("rep", "exp", None),
        P("rep", "exp", None),
        P("rep", "exp", None),
        P("rep", "exp", None, None),
        P("exp", "rep", None),
        P("exp", "rep", None),
        P("exp", "rep", None),
    )
    out_specs = (
        P("rep", "exp", None),
        P("rep", "exp", None),
        P("exp", "rep", None),
        P("exp", "rep", None),
        P("exp", "rep", None),
    )
    return jax.shard_map(body, mesh=mesh, in_specs=in_specs, out_specs=out_specs, check_vma=False)
```

profile of v0, /device:TPU:0, one launch (start us, length us, event | category | flops | bytes accessed | tf_op | source)
XLA Modules:
  0.0 239.1 jit_solution(11610807980264724344)
XLA Ops:
  7.2 0.8 copy.44
  8.3 1.1 reduce-window.6
  9.5 0.2 slice_reduce_fusion
  9.7 0.2 reduce-window.9
  10.2 0.7 fusion.18
  11.1 0.6 gather_fusion
  11.7 0.7 bitcast_select_fusion
  12.4 4.2 %all-to-all-start.1 = ((bf16[4,8,1024]{2,1,0:T(8,128)(2,1)}), bf16[4,8,1024]{2,1,0:T(8,128)(2,1)S(1)}, u32[]{:S(2)}, u32[]{:S(2)}) async-start(bf16[4,8,1024]{2,1,0:T(8,128)(2,1)} %bitcast_select_fusion), calls=%async_computation.1 | async-start | bytes 131072 | tf_op jit(solution)/shard_map/all_to_all | solution.py:54
  16.7 33.0 %all-gather.2 = bf16[1,1024,384]{2,1,0:T(8,128)(2,1)S(1)} all-gather(bf16[1,128,384]{2,1,0:T(8,128)(2,1)S(1)} %copy-done.2), channel_id=4, replica_groups=mesh['rep'=8,'exp'=4] {'rep'}, dimensions={1}, use_global_device_ids=true | all-gather | bytes 884736 | tf_op jit(solution)/shard_map/all_gather | solution.py:66
  49.7 32.4 %all-gather.1 = bf16[1,1024,384]{2,1,0:T(8,128)(2,1)S(1)} all-gather(bf16[1,128,384]{2,1,0:T(8,128)(2,1)S(1)} %copy-done.3), channel_id=3, replica_groups=mesh['rep'=8,'exp'=4] {'rep'}, dimensions={1}, use_global_device_ids=true | all-gather | bytes 884736 | tf_op jit(solution)/shard_map/all_gather | solution.py:67
  82.1 0.2 fusion.4
  82.3 0.2 fusion.7
  82.6 32.0 %all-gather = bf16[1,1024,384]{2,1,0:T(8,128)(2,1)S(1)} all-gather(bf16[1,128,384]{2,1,0:T(8,128)(2,1)S(1)} %copy-done.4), channel_id=2, replica_groups=mesh['rep'=8,'exp'=4] {'rep'}, dimensions={1}, use_global_device_ids=true | all-gather | bytes 884736 | tf_op jit(solution)/shard_map/all_gather | solution.py:68
  114.8 0.3 multiply_reduce_fusion
  115.2 7.2 %all_to_all.26 = bf16[4,1,8]{2,1,0:T(2,128)(2,1)S(1)} all-to-all(bf16[4,1,8]{2,1,0:T(2,128)(2,1)S(1)} %convert_element_type.84), channel_id=1, replica_groups=mesh['rep'=8,'exp'=4] {'exp'}, dimensions={0} | all-to-all | bytes 128 | tf_op jit(solution)/shard_map/all_to_all | solution.py:97
  122.7 6.1 %all_to_all.27 = bf16[4,1,8]{2,1,0:T(2,128)(2,1)S(1)} all-to-all(bf16[4,1,8]{2,1,0:T(2,128)(2,1)S(1)} %all_to_all.21), channel_id=1, replica_groups=mesh['rep'=8,'exp'=4] {'exp'}, dimensions={0} | all-to-all | bytes 128 | tf_op jit(solution)/shard_map/all_to_all | solution.py:61
  129.0 0.4 convolution_bitcast_fusion
  129.4 0.4 convolution_bitcast_fusion.1
  129.8 0.4 fusion.26
  130.2 2.5 %pad_maximum_fusion = f32[1024,1152]{0,1:T(8,128)} fusion(f32[1024,384]{0,1:T(8,128)S(1)} %fusion.26, f32[1024,384]{0,1:T(8,128)S(1)} %convolution_bitcast_fusion, f32[1024,384]{0,1:T(8,128)S(1)} %convolution_bitcast_fusion.1), kind=kLoop, calls=%fused_computation.2 | loop fusion | flops 2359296 | bytes 9437184 | tf_op jit(solution)/shard_map/concatenate | solution.py:114
  132.8 0.3 fusion.2
  133.1 1.0 fusion.1
  134.1 3.3 %all-to-all-start.2 = ((bf16[4,8,1024]{2,1,0:T(8,128)(2,1)}), bf16[4,8,1024]{2,1,0:T(8,128)(2,1)S(1)}, u32[]{:S(2)}, u32[]{:S(2)}) async-start(bf16[4,8,1024]{2,1,0:T(8,128)(2,1)} %fusion.1), calls=%async_computation.2 | async-start | bytes 131072 | tf_op jit(solution)/shard_map/all_to_all | solution.py:90
  137.5 0.7 copy.51
  138.1 3.3 %all-to-all-done.2 = bf16[4,8,1024]{2,1,0:T(8,128)(2,1)S(1)} async-done(((bf16[4,8,1024]{2,1,0:T(8,128)(2,1)}), bf16[4,8,1024]{2,1,0:T(8,128)(2,1)S(1)}, u32[]{:S(2)}, u32[]{:S(2)}) %all-to-all-start.2) | async-done | bytes 65568 | tf_op jit(solution)/shard_map/all_to_all | solution.py:90
  141.5 1.0 scatter_custom_fusion
  142.5 0.7 convert_bitcast_fusion
  143.3 85.4 %reduce-scatter.2.cloned.1.call-done = f32[128,1152]{0,1:T(8,128)} async-done(((f32[1024,1152]{0,1:T(8,128)}), f32[128,1152]{0,1:T(8,128)}) %reduce-scatter.2.cloned.1.call-update) | async-done | bytes 589840 | tf_op jit(solution)/shard_map/reduce_scatter | solution.py:113
  228.6 1.2 fusion.13
  229.8 0.8 copy.54
  230.6 0.8 copy.53
  231.4 0.8 copy.52
  (43 shorter events, 1.7 us)
Async XLA Ops:
  7.2 3.9 %copy-start = (bf16[1,128,1024]{2,1,0:T(8,128)(2,1)S(1)}, bf16[1,128,1024]{2,1,0:T(8,128)(2,1)}, u32[]{:S(2)}) copy-start(bf16[1,128,1024]{2,1,0:T(8,128)(2,1)} %param.9) | copy-start | bytes 786436
  7.2 9.5 %copy-start.2 = (bf16[1,128,384]{2,1,0:T(8,128)(2,1)S(1)}, bf16[1,128,384]{2,1,0:T(8,128)(2,1)}, u32[]{:S(2)}) copy-start(bf16[1,128,384]{2,1,0:T(8,128)(2,1)} %param.11) | copy-start | bytes 294916
  7.2 42.5 %copy-start.3 = (bf16[1,128,384]{2,1,0:T(8,128)(2,1)S(1)}, bf16[1,128,384]{2,1,0:T(8,128)(2,1)}, u32[]{:S(2)}) copy-start(bf16[1,128,384]{2,1,0:T(8,128)(2,1)} %param.12) | copy-start | bytes 294916
  8.2 73.9 %copy-start.1 = (bf16[1,1,32,1024]{3,2,1,0:T(8,128)(2,1)S(1)}, bf16[1,1,32,1024]{3,2,1,0:T(8,128)(2,1)}, u32[]{:S(2)}) copy-start(bf16[1,1,32,1024]{3,2,1,0:T(8,128)(2,1)} %param.10) | copy-start | bytes 196612
  12.4 102.4 %all-to-all-start.1 = ((bf16[4,8,1024]{2,1,0:T(8,128)(2,1)}), bf16[4,8,1024]{2,1,0:T(8,128)(2,1)S(1)}, u32[]{:S(2)}, u32[]{:S(2)}) async-start(bf16[4,8,1024]{2,1,0:T(8,128)(2,1)} %bitcast_select_fusion), calls=%async_computation.1 | async-start | bytes 131072 | tf_op jit(solution)/shard_map/all_to_all | solution.py:54
  16.7 65.9 %copy-start.4 = (bf16[1,128,384]{2,1,0:T(8,128)(2,1)S(1)}, bf16[1,128,384]{2,1,0:T(8,128)(2,1)}, u32[]{:S(2)}) copy-start(bf16[1,128,384]{2,1,0:T(8,128)(2,1)} %param.13) | copy-start | bytes 294916
  16.7 211.9 %reduce-scatter.2.cloned.1.call-start = ((), (), s32[]{:S(2)}) async-start(), calls=%async_computation.5 | async-start | bytes 5308416 | tf_op jit(solution)/shard_map/reduce_scatter | solution.py:113
  49.7 64.8 %copy-start.5 = (bf16[1,128,8]{1,2,0:T(8,128)(2,1)S(1)}, bf16[1,128,8]{1,2,0:T(8,128)(2,1)}, u32[]{:S(2)}) copy-start(bf16[1,128,8]{1,2,0:T(8,128)(2,1)} %param.8) | copy-start | bytes 6148
  134.1 7.4 %all-to-all-start.2 = ((bf16[4,8,1024]{2,1,0:T(8,128)(2,1)}), bf16[4,8,1024]{2,1,0:T(8,128)(2,1)S(1)}, u32[]{:S(2)}, u32[]{:S(2)}) async-start(bf16[4,8,1024]{2,1,0:T(8,128)(2,1)} %fusion.1), calls=%async_computation.2 | async-start | bytes 131072 | tf_op jit(solution)/shard_map/all_to_all | solution.py:90
Sparse Core Ops, SparseCore 0:
  132.9 95.7 reduce-scatter.1
where the time goes:
time: 240 us; the launch traced here: 239 us
  blocking collectives  111 us (46%)
  waiting for transfers between devices  88.7 us (37%)
  between operations  14.2 us (6%)
  other arithmetic  8.79 us (4%)
  starting transfers between devices  7.52 us (3%)
  local copies, waits for them, and re-layouts  5.86 us (2%)
  matrix products  3.3 us (1%)
    reduce_scatter x1, waiting for transfers between devices, body(): lax.psum_scatter(jnp.concatenate([jnp.concatenate([first_contract(inputs_...  85.4 us
    all_gather x1, blocking collectives, body(): lax.all_gather(gate_weight[0], 'rep', axis=0, tiled=True)  33 us
    all_gather x1, blocking collectives, body(): lax.all_gather(up_weight[0], 'rep', axis=0, tiled=True)  32.4 us
    all_gather x1, blocking collectives, body(): lax.all_gather(down_weight[0], 'rep', axis=0, tiled=True)  32 us
    all_to_all x1, blocking collectives, body(): lax.all_to_all(slot_route.reshape(owners, capacity), 'exp', split_axis=0,...  7.19 us
    all_to_all x1, blocking collectives, body(): lax.all_to_all(slot_scale.reshape(owners, capacity), 'exp', split_axis=0,...  6.08 us
  transfers between devices with their start and end apart: 3, of which 2 were waited for; matrix products, arithmetic and copies ran while one was open for 2% of the time, Pallas kernels for 0%

commit v1 on v0

--- a/solution.py
+++ b/solution.py
@@ -5,6 +5,22 @@
 
 TOPK = 8
 EXP_DEV = 4
+
+
+def pairwise_exchange(value, axis, split, join):
+    ways, here = (lax.axis_size(axis), lax.axis_index(axis))
+    width = value.shape[split] // ways
+    shape = list(value.shape)
+    shape[split] = width
+    height = shape[join]
+    shape[join] = height * ways
+    full = jnp.zeros(shape, value.dtype)
+    for mask in range(ways):
+        part = lax.dynamic_slice_in_dim(value, (here ^ mask) * width, width, axis=split)
+        if mask:
+            part = lax.ppermute(part, axis, [(d, d ^ mask) for d in range(ways)])
+        full = lax.dynamic_update_slice_in_dim(full, part, (here ^ mask) * height, axis=join)
+    return full
 
 
 def slot_table(block_ids, slot_count, owners):
@@ -87,13 +103,7 @@
         second_contract(gate_delta, full_gate) + second_contract(up_delta, full_up)
     ).astype(jnp.bfloat16)
     returned, returned_route = (
-        lax.all_to_all(
-            back_rows.reshape(owners, capacity, features),
-            "exp",
-            split_axis=0,
-            concat_axis=0,
-            tiled=True,
-        ),
+        pairwise_exchange(back_rows.reshape(owners, capacity, features), "exp", 0, 0),
         lax.all_to_all(
             slot_route.reshape(owners, capacity), "exp", split_axis=0, concat_axis=0, tiled=True
         ),

time: 240 us -> 239 us (level)
    all_to_all x1 -> x0, waiting for transfers between devices: 3.33 us -> none  [body(): lax.all_to_all(back_rows.reshape(owners, capacity, features), 'exp', spli...]
    all_to_all x1 -> x0, starting transfers between devices: 3.28 us -> none  [body(): lax.all_to_all(back_rows.reshape(owners, capacity, features), 'exp', spli...]
    reduce_scatter x1, waiting for transfers between devices: 85.4 us -> 88.5 us  [body(): lax.psum_scatter(jnp.concatenate([jnp.concatenate([first_contract(inputs_...]
  transfers between devices with their start and end apart: 3 -> 5, of which waited for: 2 -> 2; matrix products, arithmetic and copies ran while one was open for 2% -> 2% of each run, Pallas kernels for 0% -> 0%
where the time goes in v1:
time: 239 us
  blocking collectives  111 us (46%)
  waiting for transfers between devices  90.4 us (38%)
  between operations  14.3 us (6%)
  other arithmetic  8.79 us (4%)
  starting transfers between devices  6.44 us (3%)
  local copies, waits for them, and re-layouts  5.9 us (2%)
  matrix products  2.66 us (1%)
    reduce_scatter x1, waiting for transfers between devices, body(): lax.psum_scatter(jnp.concatenate([jnp.concatenate([first_contract(inputs_...  88.5 us
    all_gather x1, blocking collectives, body(): lax.all_gather(gate_weight[0], 'rep', axis=0, tiled=True)  33 us
    all_gather x1, blocking collectives, body(): lax.all_gather(up_weight[0], 'rep', axis=0, tiled=True)  32.4 us
    all_gather x1, blocking collectives, body(): lax.all_gather(down_weight[0], 'rep', axis=0, tiled=True)  32 us
    all_to_all x1, blocking collectives, body(): lax.all_to_all(slot_route.reshape(owners, capacity), 'exp', split_axis=0,...  7.19 us
    all_to_all x1, blocking collectives, body(): lax.all_to_all(slot_scale.reshape(owners, capacity), 'exp', split_axis=0,...  6.08 us
  transfers between devices with their start and end apart: 5, of which 2 were waited for; matrix products, arithmetic and copies ran while one was open for 2% of the time, Pallas kernels for 0%

profile of v1, /device:TPU:0, one launch (start us, length us, event | category | flops | bytes accessed | tf_op | source)
XLA Modules:
  0.0 239.1 jit_solution(14823011745648414814)
XLA Ops:
  7.2 0.8 copy.44
  8.3 1.1 reduce-window.6
  9.5 0.2 slice_reduce_fusion
  9.7 0.2 reduce-window.9
  10.2 0.7 fusion.18
  11.1 0.6 gather_fusion
  11.7 0.7 bitcast_select_fusion
  12.4 4.2 %all-to-all-start.1 = ((bf16[4,8,1024]{2,1,0:T(8,128)(2,1)}), bf16[4,8,1024]{2,1,0:T(8,128)(2,1)S(1)}, u32[]{:S(2)}, u32[]{:S(2)}) async-start(bf16[4,8,1024]{2,1,0:T(8,128)(2,1)} %bitcast_select_fusion), calls=%async_computation.1 | async-start | bytes 131072 | tf_op jit(solution)/shard_map/all_to_all | solution.py:70
  16.7 33.0 %all-gather.2 = bf16[1,1024,384]{2,1,0:T(8,128)(2,1)S(1)} all-gather(bf16[1,128,384]{2,1,0:T(8,128)(2,1)S(1)} %copy-done.2), channel_id=4, replica_groups=mesh['rep'=8,'exp'=4] {'rep'}, dimensions={1}, use_global_device_ids=true | all-gather | bytes 884736 | tf_op jit(solution)/shard_map/all_gather | solution.py:82
  49.7 32.4 %all-gather.1 = bf16[1,1024,384]{2,1,0:T(8,128)(2,1)S(1)} all-gather(bf16[1,128,384]{2,1,0:T(8,128)(2,1)S(1)} %copy-done.3), channel_id=3, replica_groups=mesh['rep'=8,'exp'=4] {'rep'}, dimensions={1}, use_global_device_ids=true | all-gather | bytes 884736 | tf_op jit(solution)/shard_map/all_gather | solution.py:83
  82.1 0.2 fusion.4
  82.3 0.2 fusion.7
  82.6 32.0 %all-gather = bf16[1,1024,384]{2,1,0:T(8,128)(2,1)S(1)} all-gather(bf16[1,128,384]{2,1,0:T(8,128)(2,1)S(1)} %copy-done.4), channel_id=2, replica_groups=mesh['rep'=8,'exp'=4] {'rep'}, dimensions={1}, use_global_device_ids=true | all-gather | bytes 884736 | tf_op jit(solution)/shard_map/all_gather | solution.py:84
  114.8 0.3 multiply_reduce_fusion
  115.2 7.2 %all_to_all.21 = bf16[4,1,8]{2,1,0:T(2,128)(2,1)S(1)} all-to-all(bf16[4,1,8]{2,1,0:T(2,128)(2,1)S(1)} %convert_element_type.84), channel_id=1, replica_groups=mesh['rep'=8,'exp'=4] {'exp'}, dimensions={0} | all-to-all | bytes 128 | tf_op jit(solution)/shard_map/all_to_all | solution.py:107
  122.7 6.1 %all_to_all.22 = bf16[4,1,8]{2,1,0:T(2,128)(2,1)S(1)} all-to-all(bf16[4,1,8]{2,1,0:T(2,128)(2,1)S(1)} %all_to_all.17), channel_id=1, replica_groups=mesh['rep'=8,'exp'=4] {'exp'}, dimensions={0} | all-to-all | bytes 128 | tf_op jit(solution)/shard_map/all_to_all | solution.py:77
  129.0 0.4 convolution_bitcast_fusion
  129.4 0.4 convolution_bitcast_fusion.1
  129.8 0.4 fusion.26
  130.2 2.5 %pad_maximum_fusion = f32[1024,1152]{0,1:T(8,128)} fusion(f32[1024,384]{0,1:T(8,128)S(1)} %fusion.26, f32[1024,384]{0,1:T(8,128)S(1)} %convolution_bitcast_fusion, f32[1024,384]{0,1:T(8,128)S(1)} %convolution_bitcast_fusion.1), kind=kLoop, calls=%fused_computation.2 | loop fusion | flops 2359296 | bytes 9437184 | tf_op jit(solution)/shard_map/concatenate | solution.py:124
  132.8 0.3 fusion.2
  133.1 0.4 fusion.1
  133.7 0.7 copy.51
  134.5 2.0 collective-permute-start.1
  136.5 1.9 collective-permute-done.1
  138.4 1.0 scatter_custom_fusion
  139.4 0.7 convert_bitcast_fusion
  140.2 88.5 %reduce-scatter.2.cloned.1.call-done = f32[128,1152]{0,1:T(8,128)} async-done(((f32[1024,1152]{0,1:T(8,128)}), f32[128,1152]{0,1:T(8,128)}) %reduce-scatter.2.cloned.1.call-update) | async-done | bytes 589840 | tf_op jit(solution)/shard_map/reduce_scatter | solution.py:123
  228.6 1.2 fusion.13
  229.8 0.8 copy.54
  230.6 0.8 copy.53
  231.4 0.8 copy.52
  (52 shorter events, 2.0 us)
Async XLA Ops:
  7.2 3.9 %copy-start = (bf16[1,128,1024]{2,1,0:T(8,128)(2,1)S(1)}, bf16[1,128,1024]{2,1,0:T(8,128)(2,1)}, u32[]{:S(2)}) copy-start(bf16[1,128,1024]{2,1,0:T(8,128)(2,1)} %param.9) | copy-start | bytes 786436
  7.2 9.5 %copy-start.2 = (bf16[1,128,384]{2,1,0:T(8,128)(2,1)S(1)}, bf16[1,128,384]{2,1,0:T(8,128)(2,1)}, u32[]{:S(2)}) copy-start(bf16[1,128,384]{2,1,0:T(8,128)(2,1)} %param.11) | copy-start | bytes 294916
  7.2 42.5 %copy-start.3 = (bf16[1,128,384]{2,1,0:T(8,128)(2,1)S(1)}, bf16[1,128,384]{2,1,0:T(8,128)(2,1)}, u32[]{:S(2)}) copy-start(bf16[1,128,384]{2,1,0:T(8,128)(2,1)} %param.12) | copy-start | bytes 294916
  8.2 73.9 %copy-start.1 = (bf16[1,1,32,1024]{3,2,1,0:T(8,128)(2,1)S(1)}, bf16[1,1,32,1024]{3,2,1,0:T(8,128)(2,1)}, u32[]{:S(2)}) copy-start(bf16[1,1,32,1024]{3,2,1,0:T(8,128)(2,1)} %param.10) | copy-start | bytes 196612
  12.4 102.4 %all-to-all-start.1 = ((bf16[4,8,1024]{2,1,0:T(8,128)(2,1)}), bf16[4,8,1024]{2,1,0:T(8,128)(2,1)S(1)}, u32[]{:S(2)}, u32[]{:S(2)}) async-start(bf16[4,8,1024]{2,1,0:T(8,128)(2,1)} %bitcast_select_fusion), calls=%async_computation.1 | async-start | bytes 131072 | tf_op jit(solution)/shard_map/all_to_all | solution.py:70
  16.7 65.9 %copy-start.4 = (bf16[1,128,384]{2,1,0:T(8,128)(2,1)S(1)}, bf16[1,128,384]{2,1,0:T(8,128)(2,1)}, u32[]{:S(2)}) copy-start(bf16[1,128,384]{2,1,0:T(8,128)(2,1)} %param.13) | copy-start | bytes 294916
  16.7 211.9 %reduce-scatter.2.cloned.1.call-start = ((), (), s32[]{:S(2)}) async-start(), calls=%async_computation.4 | async-start | bytes 5308416 | tf_op jit(solution)/shard_map/reduce_scatter | solution.py:123
  49.7 64.8 %copy-start.5 = (bf16[1,128,8]{1,2,0:T(8,128)(2,1)S(1)}, bf16[1,128,8]{1,2,0:T(8,128)(2,1)}, u32[]{:S(2)}) copy-start(bf16[1,128,8]{1,2,0:T(8,128)(2,1)} %param.8) | copy-start | bytes 6148
  133.5 3.0 %collective-permute-start = (bf16[1,8,1024]{2,1,0:T(8,128)(2,1)S(1)}, bf16[1,8,1024]{2,1,0:T(8,128)(2,1)S(1)}, u32[]{:S(2)}, u32[]{:S(2)}) collective-permute-start(bf16[1,8,1024]{2,1,0:T(8,128)(2,1)S(1)} %get-tuple-element.43), channel_id=1, source_target_pairs={{0,1},{1,0},{2,3},{3,2},{4,5},{5,4},{6,7},{7,6},{8,9},{9,8},{10,11... | collective-permute-start | bytes 49160 | tf_op jit(solution)/shard_map/ppermute | solution.py:21
  134.3 4.0 %collective-permute-start.2 = (bf16[1,8,1024]{2,1,0:T(8,128)(2,1)S(1)}, bf16[1,8,1024]{2,1,0:T(8,128)(2,1)S(1)}, u32[]{:S(2)}, u32[]{:S(2)}) collective-permute-start(bf16[1,8,1024]{2,1,0:T(8,128)(2,1)S(1)} %get-tuple-element.41), channel_id=1, source_target_pairs={{0,3},{1,2},{2,1},{3,0},{4,7},{5,6},{6,5},{7,4},{8,11},{9,10},{10,... | collective-permute-start | bytes 49160 | tf_op jit(solution)/shard_map/ppermute | solution.py:21
  134.5 3.9 %collective-permute-start.1 = (bf16[1,8,1024]{2,1,0:T(8,128)(2,1)S(1)}, bf16[1,8,1024]{2,1,0:T(8,128)(2,1)S(1)}, u32[]{:S(2)}, u32[]{:S(2)}) collective-permute-start(bf16[1,8,1024]{2,1,0:T(8,128)(2,1)S(1)} %get-tuple-element.42), channel_id=1, source_target_pairs={{0,2},{1,3},{2,0},{3,1},{4,6},{5,7},{6,4},{7,5},{8,10},{9,11},{10,... | collective-permute-start | bytes 49160 | tf_op jit(solution)/shard_map/ppermute | solution.py:21
Sparse Core Ops, SparseCore 0:
  132.9 95.7 reduce-scatter.1
